TPU v7x, 256 devices: a whole 4x4x8 slice. The times are simulated.
256 devices in a mesh: st: 128 (over z, x_lo, y, core), row: 2 (over x_hi).
Axes of the slice: x: 4 (x_hi: 2, x_lo: 2; x = x_hi * 2 + x_lo), y: 4, z: 8, core: 2. Of those that a mesh axis runs over, the one named last changes fastest.
Arguments:
- forcing: bfloat16 [2, 128, 1024, 256], P(None, 'st', 'row'), may hold values from -6 to 6
- inverse_first: bfloat16 [2, 128, 1024, 1024], P(None, 'st', 'row'), may hold values from -0.1875 to 0.1875
- lower_first: bfloat16 [2, 128, 1024, 1024], P(None, 'st', 'row'), may hold values from -0.1875 to 0.1875
- upper_first: bfloat16 [2, 128, 1024, 1024], P(None, 'st', 'row'), may hold values from -0.1875 to 0.1875
- inverse_second: bfloat16 [2, 128, 1024, 1024], P(None, 'st', 'row'), may hold values from -0.1875 to 0.1875
- lower_second: bfloat16 [2, 128, 1024, 1024], P(None, 'st', 'row'), may hold values from -0.1875 to 0.1875
- upper_second: bfloat16 [2, 128, 1024, 1024], P(None, 'st', 'row'), may hold values from -0.1875 to 0.1875
Outputs:
- reduced_forcing: bfloat16 [2, 128, 1024, 256], P(None, 'st', 'row')
All inputs are finite; a program needn't handle non-finite values.
Results may differ from a plain program's by a relative error of at most 0.0059.
Values may be sent and summed in bfloat16 or wider, within the bound.
No kernel may reach another device: no remote copies, remote signals or barrier semaphores. Data moves between devices by JAX's collectives and lax.ppermute only.
A program may use at most 64 MiB of HBM per device.

v0:
```python
import jax
import jax.numpy as jnp
from jax import lax
from jax.sharding import PartitionSpec as P


def from_behind(value, axis, steps):
    count = lax.axis_size(axis)
    pairs = [(source, (source + steps) % count) for source in range(count)]
    return lax.ppermute(value, axis, pairs)


def shifted_earlier(received, stride):
    position = lax.axis_index("st")
    earlier = jnp.concatenate([jnp.zeros_like(received[:1]), received[:-1]], axis=0)
    return jnp.where(position < stride, earlier, received)


def shifted_later(received, stride):
    position = lax.axis_index("st")
    later_rows = jnp.concatenate([received[1:], jnp.zeros_like(received[:1])], axis=0)
    return jnp.where(position >= lax.axis_size("st") - stride, later_rows, received)


def product(blocks, vectors):
    return jnp.einsum("jrk,jkc->jrc", blocks, vectors, preferred_element_type=jnp.float32)


def reduce_level(forcing_now, inverse, lower, upper, stride):
    scaled = product(inverse, lax.all_gather(forcing_now, "row", axis=1, tiled=True)).astype(
        jnp.bfloat16
    )
    gathered = lax.all_gather(scaled, "row", axis=1, tiled=True)
    from_below = shifted_earlier(from_behind(gathered, "st", stride), stride)
    from_above = shifted_later(from_behind(gathered, "st", -stride), stride)
    coupled = product(lower, from_below) + product(upper, from_above)
    return (forcing_now.astype(jnp.float32) - coupled).astype(jnp.bfloat16)


def on_device(
    forcing, inverse_first, lower_first, upper_first, inverse_second, lower_second, upper_second
):

    def squeeze(array):
        return array.reshape((array.shape[0],) + array.shape[2:])

    forcing_first = reduce_level(
        squeeze(forcing), squeeze(inverse_first), squeeze(lower_first), squeeze(upper_first), 1
    )
    reduced = reduce_level(
        forcing_first, squeeze(inverse_second), squeeze(lower_second), squeeze(upper_second), 2
    )
    return reduced.reshape(forcing.shape)


def solution(mesh):
    return jax.shard_map(
        on_device,
        mesh=mesh,
        in_specs=(
            P(None, "st", "row", None),
            P(None, "st", "row", None),
            P(None, "st", "row", None),
            P(None, "st", "row", None),
            P(None, "st", "row", None),
            P(None, "st", "row", None),
            P(None, "st", "row", None),
        ),
        out_specs=P(None, "st", "row", None),
        check_vma=False,
    )
```

profile of v0, /device:TPU:1, one launch (start us, length us, event | category | flops | bytes accessed | tf_op | source)
XLA Modules:
  0.0 201.1 jit_solution(2558496426390451680)
XLA Ops:
  6.5 0.0 copy-start
  6.5 0.0 all-gather.12.cloned.1.call-start
  6.5 0.7 all-gather.12.cloned.1.call-update
  7.3 0.0 copy-start.1
  7.3 0.0 all-gather.6.cloned.1.call-start
  7.3 33.3 %all-gather.12.cloned.1.call-done = bf16[2,1,1024,256]{3,2,0,1:T(8,128)(2,1)} async-done(((bf16[2,1,512,256]{3,2,0,1:T(8,128)(2,1)}), bf16[2,1,1024,256]{3,2,0,1:T(8,128)(2,1)}) %all-gather.12.cloned.1.call-update) | async-done | bytes 1048592 | tf_op jit(solution)/shard_map/all_gather | solution.py:30
  40.6 0.0 copy-done
  40.7 2.7 %fusion.27 = bf16[2,512,256]{2,1,0:T(8,128)(2,1)} fusion(bf16[2,1,512,1024]{3,2,1,0:T(8,128)(2,1)S(1)} %copy-done, bf16[2,1,1024,256]{3,2,0,1:T(8,128)(2,1)} %all-gather.12.cloned.1.call-done), kind=kOutput, calls=%fused_computation.17 | convolution fusion | flops 537133056 | bytes 3670016 | tf_op jit(solution)/shard_map/jrk,jkc->jrc/dot_general | solution.py:26
  43.4 0.0 all-gather.6.cloned.1.call-update
  43.4 0.0 all-gather.8.cloned.1.call-start
  43.5 27.4 %all-gather.6.cloned.1.call-done = bf16[2,1024,256]{2,1,0:T(8,128)(2,1)} async-done(((bf16[2,512,256]{2,1,0:T(8,128)(2,1)}), bf16[2,1024,256]{2,1,0:T(8,128)(2,1)}) %all-gather.6.cloned.1.call-update) | async-done | bytes 1048592 | tf_op jit(solution)/shard_map/all_gather | solution.py:33
  70.9 0.8 collective-permute-start.1
  71.7 1.1 collective-permute-start
  72.8 0.0 copy-done.1
  72.8 0.2 copy.8
  73.1 12.9 %collective-permute-done.1 = bf16[2,1024,256]{2,1,0:T(8,128)(2,1)} collective-permute-done((bf16[2,1024,256]{2,1,0:T(8,128)(2,1)}, bf16[2,1024,256]{2,1,0:T(8,128)(2,1)}, u32[]{:S(2)}, u32[]{:S(2)}) %collective-permute-start.1) | collective-permute-done | bytes 1048608 | tf_op jit(solution)/shard_map/ppermute | solution.py:10
  85.9 1.1 slice.17
  87.0 0.0 collective-permute-done
  87.0 1.1 slice.16
  88.1 0.0 copy-start.4
  88.1 2.9 %fusion.6 = f32[2,256,512]{2,1,0:T(8,128)S(1)} fusion(bf16[2,1,512,1024]{3,2,1,0:T(8,128)(2,1)} %param.10, bf16[2,1024,256]{2,1,0:T(8,128)(2,1)} %collective-permute-done.1, bf16[1,1024,256]{2,1,0:T(8,128)(2,1)S(1)} %slice.17, pred[]{:T(512)S(6)} %ge.6), kind=kOutput, calls=%fused_computation.6 | convolution fusion | flops 537395200 | bytes 4718593 | tf_op jit(solution)/shard_map/jrk,jkc->jrc/dot_general | solution.py:26
  91.1 0.0 copy-done.4
  91.1 3.1 %fusion.33 = bf16[2,512,256]{1,2,0:T(8,128)(2,1)} fusion(f32[2,256,512]{2,1,0:T(8,128)S(1)} %fusion.6, bf16[2,1,512,1024]{3,2,1,0:T(8,128)(2,1)S(1)} %copy-done.4, bf16[2,1024,256]{2,1,0:T(8,128)(2,1)} %collective-permute-done, bf16[1,1024,256]{2,1,0:T(8,128)(2,1)S(1)} %slice.16, pred[]{:T(512)S(6)} %lt.6, bf16[2,1,512,256]{2,3,0,1:T(8,128)(2,1)S(1)} %copy.8), kind=kOutput, calls=%fused_computation.19 | convolution fusion | flops 538443776 | bytes 5767169 | tf_op jit(solution)/shard_map/jrk,jkc->jrc/dot_general | solution.py:26
  94.2 0.0 all-gather.8.cloned.1.call-update
  94.2 0.0 all-gather.10.cloned.1.call-start
  94.3 30.5 %all-gather.8.cloned.1.call-done = bf16[2,1024,256]{1,2,0:T(8,128)(2,1)} async-done(((bf16[2,512,256]{1,2,0:T(8,128)(2,1)}), bf16[2,1024,256]{1,2,0:T(8,128)(2,1)}) %all-gather.8.cloned.1.call-update) | async-done | bytes 1048592 | tf_op jit(solution)/shard_map/all_gather | solution.py:30
  124.7 3.5 %fusion.36 = bf16[2,512,256]{1,2,0:T(8,128)(2,1)} fusion(bf16[2,1024,256]{1,2,0:T(8,128)(2,1)} %all-gather.8.cloned.1.call-done, bf16[2,1,512,1024]{3,2,1,0:T(8,128)(2,1)} %param.11), kind=kOutput, calls=%fused_computation.20 | convolution fusion | flops 537133056 | bytes 3670016 | tf_op jit(solution)/shard_map/jrk,jkc->jrc/dot_general | solution.py:26
  128.2 0.0 all-gather.10.cloned.1.call-update
  128.2 27.5 %all-gather.10.cloned.1.call-done = bf16[2,1024,256]{1,2,0:T(8,128)(2,1)} async-done(((bf16[2,512,256]{1,2,0:T(8,128)(2,1)}), bf16[2,1024,256]{1,2,0:T(8,128)(2,1)}) %all-gather.10.cloned.1.call-update) | async-done | bytes 1048592 | tf_op jit(solution)/shard_map/all_gather | solution.py:33
  155.7 5.2 %collective-permute-start.3 = (bf16[2,1024,256]{1,2,0:T(8,128)(2,1)}, bf16[2,1024,256]{1,2,0:T(8,128)(2,1)}, u32[]{:S(2)}, u32[]{:S(2)}) collective-permute-start(bf16[2,1024,256]{1,2,0:T(8,128)(2,1)} %all-gather.10.cloned.1.call-done), channel_id=1, source_target_pairs={{0,252},{2,254},{4,0},{6,2},{8,4},{10,6},{12,8},{14,10},{16,12},{1... | collective-permute-start | bytes 3145736 | tf_op jit(solution)/shard_map/ppermute | solution.py:10
  161.0 0.0 collective-permute-start.2
  161.0 22.0 %collective-permute-done.3 = bf16[2,1024,256]{1,2,0:T(8,128)(2,1)} collective-permute-done((bf16[2,1024,256]{1,2,0:T(8,128)(2,1)}, bf16[2,1024,256]{1,2,0:T(8,128)(2,1)}, u32[]{:S(2)}, u32[]{:S(2)}) %collective-permute-start.3) | collective-permute-done | bytes 1048608 | tf_op jit(solution)/shard_map/ppermute | solution.py:10
  182.9 1.1 slice.19
  184.0 5.0 %collective-permute-done.2 = bf16[2,1024,256]{1,2,0:T(8,128)(2,1)S(1)} collective-permute-done((bf16[2,1024,256]{1,2,0:T(8,128)(2,1)}, bf16[2,1024,256]{1,2,0:T(8,128)(2,1)S(1)}, u32[]{:S(2)}, u32[]{:S(2)}) %collective-permute-start.2) | collective-permute-done | bytes 1048608 | tf_op jit(solution)/shard_map/ppermute | solution.py:10
  189.0 0.0 copy-start.3
  189.0 0.9 copy-done.3
  190.0 0.0 copy-start.2
  190.0 0.0 copy-start.5
  190.0 2.8 %fusion = f32[2,256,512]{2,1,0:T(8,128)S(1)} fusion(bf16[2,1,512,1024]{3,2,1,0:T(8,128)(2,1)} %param.13, bf16[2,1024,256]{1,2,0:T(8,128)(2,1)} %collective-permute-done.3, bf16[1,1024,256]{1,2,0:T(8,128)(2,1)S(1)} %slice.19, pred[]{:T(512)S(6)} %ge.7), kind=kOutput, calls=%fused_computation | convolution fusion | flops 537395200 | bytes 4718593 | tf_op jit(solution)/shard_map/jrk,jkc->jrc/dot_general | solution.py:26
  192.8 0.0 copy-done.2
  192.8 0.0 copy-done.5
  192.8 0.8 fusion.54
  193.6 1.0 copy.12
  (1 shorter events, 0.0 us)
Async XLA Ops:
  6.5 34.1 %copy-start = (bf16[2,1,512,1024]{3,2,1,0:T(8,128)(2,1)S(1)}, bf16[2,1,512,1024]{3,2,1,0:T(8,128)(2,1)}, u32[]{:S(2)}) copy-start(bf16[2,1,512,1024]{3,2,1,0:T(8,128)(2,1)} %param.8) | copy-start | bytes 6291460
  6.5 34.1 %all-gather.12.cloned.1.call-start = ((), (), s32[]{:S(2)}) async-start(), calls=%async_computation.3 | async-start | bytes 1572864 | tf_op jit(solution)/shard_map/all_gather | solution.py:30
  7.3 65.6 %copy-start.1 = (bf16[2,1,512,256]{3,2,1,0:T(8,128)(2,1)S(1)}, bf16[2,1,512,256]{3,2,1,0:T(8,128)(2,1)}, u32[]{:S(2)}) copy-start(bf16[2,1,512,256]{3,2,1,0:T(8,128)(2,1)} %param.7) | copy-start | bytes 1572868
  7.3 63.6 %all-gather.6.cloned.1.call-start = ((), (), s32[]{:S(2)}) async-start(), calls=%async_computation | async-start | bytes 1572864 | tf_op jit(solution)/shard_map/all_gather | solution.py:33
  43.4 81.3 %all-gather.8.cloned.1.call-start = ((), (), s32[]{:S(2)}) async-start(), calls=%async_computation.1 | async-start | bytes 1572864 | tf_op jit(solution)/shard_map/all_gather | solution.py:30
  70.9 15.0 %collective-permute-start.1 = (bf16[2,1024,256]{2,1,0:T(8,128)(2,1)}, bf16[2,1024,256]{2,1,0:T(8,128)(2,1)}, u32[]{:S(2)}, u32[]{:S(2)}) collective-permute-start(bf16[2,1024,256]{2,1,0:T(8,128)(2,1)} %all-gather.6.cloned.1.call-done), channel_id=1, source_target_pairs={{0,254},{2,0},{4,2},{6,4},{8,6},{10,8},{12,10},{14,12},{16,14},{18... | collective-permute-start | bytes 3145736 | tf_op jit(solution)/shard_map/ppermute | solution.py:10
  71.7 15.3 %collective-permute-start = (bf16[2,1024,256]{2,1,0:T(8,128)(2,1)}, bf16[2,1024,256]{2,1,0:T(8,128)(2,1)}, u32[]{:S(2)}, u32[]{:S(2)}) collective-permute-start(bf16[2,1024,256]{2,1,0:T(8,128)(2,1)} %all-gather.6.cloned.1.call-done), channel_id=1, source_target_pairs={{0,2},{2,4},{4,6},{6,8},{8,10},{10,12},{12,14},{14,16},{16,18},{18... | collective-permute-start | bytes 3145736 | tf_op jit(solution)/shard_map/ppermute | solution.py:10
  88.1 3.0 %copy-start.4 = (bf16[2,1,512,1024]{3,2,1,0:T(8,128)(2,1)S(1)}, bf16[2,1,512,1024]{3,2,1,0:T(8,128)(2,1)}, u32[]{:S(2)}) copy-start(bf16[2,1,512,1024]{3,2,1,0:T(8,128)(2,1)} %param.9) | copy-start | bytes 6291460
  94.2 61.5 %all-gather.10.cloned.1.call-start = ((), (), s32[]{:S(2)}) async-start(), calls=%async_computation.2 | async-start | bytes 1572864 | tf_op jit(solution)/shard_map/all_gather | solution.py:33
  155.7 27.2 %collective-permute-start.3 = (bf16[2,1024,256]{1,2,0:T(8,128)(2,1)}, bf16[2,1024,256]{1,2,0:T(8,128)(2,1)}, u32[]{:S(2)}, u32[]{:S(2)}) collective-permute-start(bf16[2,1024,256]{1,2,0:T(8,128)(2,1)} %all-gather.10.cloned.1.call-done), channel_id=1, source_target_pairs={{0,252},{2,254},{4,0},{6,2},{8,4},{10,6},{12,8},{14,10},{16,12},{1... | collective-permute-start | bytes 3145736 | tf_op jit(solution)/shard_map/ppermute | solution.py:10
  161.0 28.0 %collective-permute-start.2 = (bf16[2,1024,256]{1,2,0:T(8,128)(2,1)}, bf16[2,1024,256]{1,2,0:T(8,128)(2,1)S(1)}, u32[]{:S(2)}, u32[]{:S(2)}) collective-permute-start(bf16[2,1024,256]{1,2,0:T(8,128)(2,1)} %all-gather.10.cloned.1.call-done), channel_id=1, source_target_pairs={{0,4},{2,6},{4,8},{6,10},{8,12},{10,14},{12,16},{14,18},{16,20},{1... | collective-permute-start | bytes 3145736 | tf_op jit(solution)/shard_map/ppermute | solution.py:10
  189.0 1.0 copy-start.3
  190.0 2.8 %copy-start.2 = (bf16[2,512,256]{1,2,0:T(8,128)(2,1)S(1)}, bf16[2,512,256]{1,2,0:T(8,128)(2,1)}, u32[]{:S(2)}) copy-start(bf16[2,512,256]{1,2,0:T(8,128)(2,1)} %fusion.33) | copy-start | bytes 1572868
  190.0 2.8 %copy-start.5 = (bf16[2,1,512,1024]{3,2,1,0:T(8,128)(2,1)S(1)}, bf16[2,1,512,1024]{3,2,1,0:T(8,128)(2,1)}, u32[]{:S(2)}) copy-start(bf16[2,1,512,1024]{3,2,1,0:T(8,128)(2,1)} %param.12) | copy-start | bytes 6291460
Sparse Core Ops, SparseCore 0:
  9.1 31.4 all-gather.11
  43.5 27.3 all-gather.5
  94.4 30.3 all-gather.7
  128.4 27.3 all-gather.9
where the time goes:
time: 201 us
  waiting for transfers between devices  159 us (79%)
  matrix products  15.9 us (8%)
  between operations  13.2 us (7%)
  starting transfers between devices  7.28 us (4%)
  local copies, waits for them, and re-layouts  5.44 us (3%)
    all_gather x2, waiting for transfers between devices, reduce_level(): lax.all_gather(forcing_now, 'row', axis=1, tiled=True)  63.8 us
    all_gather x2, waiting for transfers between devices, reduce_level(): gathered = lax.all_gather(scaled, 'row', axis=1, tiled=True)  54.9 us
    ppermute x4, waiting for transfers between devices, from_behind(): return lax.ppermute(value, axis, pairs)  39.8 us
    dot_general x6, matrix products, product(): jnp.einsum('jrk,jkc->jrc', blocks, vectors, preferred_element_type=jnp.fl...  15.9 us
    ppermute x4, starting transfers between devices, from_behind(): return lax.ppermute(value, axis, pairs)  7.15 us
  transfers between devices with their start and end apart: 8, of which 7 were waited for; matrix products, arithmetic and copies ran while one was open for 1% of the time, Pallas kernels for 0%

commit v1 on v0

--- a/solution.py
+++ b/solution.py
@@ -2,6 +2,11 @@
 import jax.numpy as jnp
 from jax import lax
 from jax.sharding import PartitionSpec as P
+
+
+def gather_over(array, axis, along):
+    sent = jnp.stack([array] * lax.axis_size(axis))
+    return jnp.concatenate(lax.all_to_all(sent, axis, 0, 0), axis=along)
 
 
 def from_behind(value, axis, steps):
@@ -30,7 +35,7 @@
     scaled = product(inverse, lax.all_gather(forcing_now, "row", axis=1, tiled=True)).astype(
         jnp.bfloat16
     )
-    gathered = lax.all_gather(scaled, "row", axis=1, tiled=True)
+    gathered = gather_over(scaled, "row", 1)
     from_below = shifted_earlier(from_behind(gathered, "st", stride), stride)
     from_above = shifted_later(from_behind(gathered, "st", -stride), stride)
     coupled = product(lower, from_below) + product(upper, from_above)

time: 201 us -> 181 us (0.900)
  waiting for transfers between devices: 159 us -> 102 us
  blocking collectives: 0 us -> 33.7 us
  local copies, waits for them, and re-layouts: 5.44 us -> 7.9 us
    all_gather x2 -> x0, waiting for transfers between devices: 54.9 us -> none  [reduce_level(): gathered = lax.all_gather(scaled, 'row', axis=1, tiled=True)]
    all_to_all x0 -> x2, blocking collectives: none -> 33.7 us  [gather_over(): return jnp.concatenate(lax.all_to_all(sent, axis, 0, 0), axis=along)]
    reshape x0 -> x2, local copies, waits for them, and re-layouts: none -> 2.36 us  [gather_over(): return jnp.concatenate(lax.all_to_all(sent, axis, 0, 0), axis=along)]
  transfers between devices with their start and end apart: 8 -> 6, of which waited for: 7 -> 5; matrix products, arithmetic and copies ran while one was open for 1% -> 1% of each run, Pallas kernels for 0% -> 0%
where the time goes in v1:
time: 181 us
  waiting for transfers between devices  102 us (56%)
  blocking collectives  33.7 us (19%)
  matrix products  15.5 us (9%)
  between operations  13.5 us (7%)
  starting transfers between devices  8.01 us (4%)
  local copies, waits for them, and re-layouts  7.9 us (4%)
    all_gather x2, waiting for transfers between devices, reduce_level(): lax.all_gather(forcing_now, 'row', axis=1, tiled=True)  62.1 us
    ppermute x4, waiting for transfers between devices, from_behind(): return lax.ppermute(value, axis, pairs)  38.9 us
    all_to_all x2, blocking collectives, gather_over(): return jnp.concatenate(lax.all_to_all(sent, axis, 0, 0), axis=along)  33.7 us
    dot_general x6, matrix products, product(): jnp.einsum('jrk,jkc->jrc', blocks, vectors, preferred_element_type=jnp.fl...  15.5 us
    ppermute x4, starting transfers between devices, from_behind(): return lax.ppermute(value, axis, pairs)  7.97 us
  transfers between devices with their start and end apart: 6, of which 5 were waited for; matrix products, arithmetic and copies ran while one was open for 1% of the time, Pallas kernels for 0%

profile of v1, /device:TPU:1, one launch (start us, length us, event | category | flops | bytes accessed | tf_op | source)
XLA Modules:
  0.0 180.6 jit_solution(16584724243607088121)
XLA Ops:
  6.5 0.0 copy-start
  6.5 0.0 all-gather.6.cloned.1.call-start
  6.5 0.7 all-gather.6.cloned.1.call-update
  7.3 0.0 all-gather.4.cloned.1.call-start
  7.3 33.3 %all-gather.6.cloned.1.call-done = bf16[2,1,1024,256]{3,2,0,1:T(8,128)(2,1)} async-done(((bf16[2,1,512,256]{3,2,0,1:T(8,128)(2,1)}), bf16[2,1,1024,256]{3,2,0,1:T(8,128)(2,1)}) %all-gather.6.cloned.1.call-update) | async-done | bytes 1048592 | tf_op jit(solution)/shard_map/all_gather | solution.py:35
  40.6 0.0 copy-done
  40.7 1.9 %fusion.39 = bf16[1,2,512,256]{3,2,1,0:T(8,128)(2,1)S(1)} fusion(bf16[2,1,512,1024]{3,2,1,0:T(8,128)(2,1)S(1)} %copy-done, bf16[2,1,1024,256]{3,2,0,1:T(8,128)(2,1)} %all-gather.6.cloned.1.call-done), kind=kOutput, calls=%fused_computation.21 | convolution fusion | flops 537133056 | bytes 3670016 | tf_op jit(solution)/shard_map/jrk,jkc->jrc/dot_general | solution.py:31
  42.6 0.1 pad_maximum_fusion
  42.7 0.0 copy-start.3
  42.7 16.9 %all_to_all.10 = bf16[2,2,512,256]{3,2,1,0:T(8,128)(2,1)S(1)} all-to-all(bf16[2,2,512,256]{3,2,1,0:T(8,128)(2,1)S(1)} %pad_maximum_fusion), channel_id=1, replica_groups=mesh['st'=128,'row'=2] {'row'}, dimensions={0} | all-to-all | bytes 2097152 | tf_op jit(solution)/shard_map/all_to_all | solution.py:9
  59.6 1.1 copy.13
  60.7 1.7 collective-permute-start.1
  62.4 1.1 collective-permute-start
  63.5 0.0 copy-done.3
  63.5 0.2 copy.11
  63.7 12.9 %collective-permute-done.1 = bf16[2,1024,256]{2,1,0:T(8,128)(2,1)} collective-permute-done((bf16[2,1024,256]{2,1,0:T(8,128)(2,1)}, bf16[2,1024,256]{2,1,0:T(8,128)(2,1)}, u32[]{:S(2)}, u32[]{:S(2)}) %collective-permute-start.1) | collective-permute-done | bytes 1048608 | tf_op jit(solution)/shard_map/ppermute | solution.py:15
  76.6 1.1 slice.17
  77.6 0.0 collective-permute-done
  77.7 1.1 slice.16
  78.7 0.0 copy-start.4
  78.7 2.9 %fusion.6 = f32[2,256,512]{2,1,0:T(8,128)S(1)} fusion(bf16[2,1,512,1024]{3,2,1,0:T(8,128)(2,1)} %param.10, bf16[2,1024,256]{2,1,0:T(8,128)(2,1)} %collective-permute-done.1, bf16[1,1024,256]{2,1,0:T(8,128)(2,1)S(1)} %slice.17, pred[]{:T(512)S(6)} %ge.6), kind=kOutput, calls=%fused_computation.6 | convolution fusion | flops 537395200 | bytes 4718593 | tf_op jit(solution)/shard_map/jrk,jkc->jrc/dot_general | solution.py:31
  81.7 0.0 copy-done.4
  81.7 3.1 %fusion.33 = bf16[2,512,256]{1,2,0:T(8,128)(2,1)} fusion(f32[2,256,512]{2,1,0:T(8,128)S(1)} %fusion.6, bf16[2,1,512,1024]{3,2,1,0:T(8,128)(2,1)S(1)} %copy-done.4, bf16[2,1024,256]{2,1,0:T(8,128)(2,1)} %collective-permute-done, bf16[1,1024,256]{2,1,0:T(8,128)(2,1)S(1)} %slice.16, pred[]{:T(512)S(6)} %lt.6, bf16[2,1,512,256]{2,3,0,1:T(8,128)(2,1)S(1)} %copy.11), kind=kOutput, calls=%fused_computation.19 | convolution fusion | flops 538443776 | bytes 5767169 | tf_op jit(solution)/shard_map/jrk,jkc->jrc/dot_general | solution.py:31
  84.9 0.0 all-gather.4.cloned.1.call-update
  84.9 28.7 %all-gather.4.cloned.1.call-done = bf16[2,1024,256]{1,2,0:T(8,128)(2,1)} async-done(((bf16[2,512,256]{1,2,0:T(8,128)(2,1)}), bf16[2,1024,256]{1,2,0:T(8,128)(2,1)}) %all-gather.4.cloned.1.call-update) | async-done | bytes 1048592 | tf_op jit(solution)/shard_map/all_gather | solution.py:35
  113.6 2.7 %fusion.36 = bf16[1,2,512,256]{2,3,1,0:T(8,128)(2,1)S(1)} fusion(bf16[2,1024,256]{1,2,0:T(8,128)(2,1)} %all-gather.4.cloned.1.call-done, bf16[2,1,512,1024]{3,2,1,0:T(8,128)(2,1)} %param.11), kind=kOutput, calls=%fused_computation.20 | convolution fusion | flops 537133056 | bytes 3670016 | tf_op jit(solution)/shard_map/jrk,jkc->jrc/dot_general | solution.py:31
  116.3 0.1 pad_maximum_fusion.1
  116.4 16.8 %all_to_all.11 = bf16[2,2,512,256]{2,3,1,0:T(8,128)(2,1)S(1)} all-to-all(bf16[2,2,512,256]{2,3,1,0:T(8,128)(2,1)S(1)} %pad_maximum_fusion.1), channel_id=1, replica_groups=mesh['st'=128,'row'=2] {'row'}, dimensions={0} | all-to-all | bytes 2097152 | tf_op jit(solution)/shard_map/all_to_all | solution.py:9
  133.2 1.3 copy.16
  134.5 5.2 %collective-permute-start.3 = (bf16[2,1024,256]{2,1,0:T(8,128)(2,1)}, bf16[2,1024,256]{2,1,0:T(8,128)(2,1)}, u32[]{:S(2)}, u32[]{:S(2)}) collective-permute-start(bf16[2,1024,256]{2,1,0:T(8,128)(2,1)} %bitcast.77), channel_id=1, source_target_pairs={{0,252},{2,254},{4,0},{6,2},{8,4},{10,6},{12,8},{14,10},{16,12},{1... | collective-permute-start | bytes 3145736 | tf_op jit(solution)/shard_map/ppermute | solution.py:15
  139.7 0.0 collective-permute-start.2
  139.7 21.1 %collective-permute-done.3 = bf16[2,1024,256]{2,1,0:T(8,128)(2,1)} collective-permute-done((bf16[2,1024,256]{2,1,0:T(8,128)(2,1)}, bf16[2,1024,256]{2,1,0:T(8,128)(2,1)}, u32[]{:S(2)}, u32[]{:S(2)}) %collective-permute-start.3) | collective-permute-done | bytes 1048608 | tf_op jit(solution)/shard_map/ppermute | solution.py:15
  160.8 1.1 slice.19
  161.8 5.0 %collective-permute-done.2 = bf16[2,1024,256]{2,1,0:T(8,128)(2,1)S(1)} collective-permute-done((bf16[2,1024,256]{2,1,0:T(8,128)(2,1)}, bf16[2,1024,256]{2,1,0:T(8,128)(2,1)S(1)}, u32[]{:S(2)}, u32[]{:S(2)}) %collective-permute-start.2) | collective-permute-done | bytes 1048608 | tf_op jit(solution)/shard_map/ppermute | solution.py:15
  166.8 0.0 copy-start.1
  166.8 0.0 copy-start.2
  166.9 3.0 %fusion = f32[2,256,512]{2,1,0:T(8,128)S(1)} fusion(bf16[2,1,512,1024]{3,2,1,0:T(8,128)(2,1)} %param.13, bf16[2,1024,256]{2,1,0:T(8,128)(2,1)} %collective-permute-done.3, bf16[1,1024,256]{2,1,0:T(8,128)(2,1)S(1)} %slice.19, pred[]{:T(512)S(6)} %ge.7), kind=kOutput, calls=%fused_computation | convolution fusion | flops 537395200 | bytes 4718593 | tf_op jit(solution)/shard_map/jrk,jkc->jrc/dot_general | solution.py:31
  169.8 0.0 copy-done.1
  169.8 0.0 copy-done.2
  169.8 1.9 %fusion.57 = bf16[2,1,512,256]{2,3,0,1:T(8,128)(2,1)} fusion(f32[2,256,512]{2,1,0:T(8,128)S(1)} %fusion, bf16[2,1,512,1024]{3,2,1,0:T(8,128)(2,1)S(1)} %copy-done.1, bf16[2,1024,256]{2,1,0:T(8,128)(2,1)S(1)} %collective-permute-done.2, bf16[1,1024,256]{2,1,0:T(8,128)(2,1)S(1)} %slice.18, pred[]{:T(512)S(6)} %lt.7, bf16[2,512,256]{1,2,0:T(8,128)(2,1)S(1)} %copy-done.2), kind=kOutput, calls=%fused_computation.36 | convolution fusion | flops 538443776 | bytes 5767169 | tf_op jit(solution)/shard_map/jrk,jkc->jrc/dot_general | solution.py:31
  171.7 2.0 %copy.19 = bf16[2,1,512,256]{3,2,1,0:T(8,128)(2,1)} copy(bf16[2,1,512,256]{2,3,0,1:T(8,128)(2,1)} %fusion.57) | data formatting | bytes 1048576 | tf_op jit(solution)/shard_map/reshape | solution.py:58
  (1 shorter events, 0.0 us)
Async XLA Ops:
  6.5 34.1 %copy-start = (bf16[2,1,512,1024]{3,2,1,0:T(8,128)(2,1)S(1)}, bf16[2,1,512,1024]{3,2,1,0:T(8,128)(2,1)}, u32[]{:S(2)}) copy-start(bf16[2,1,512,1024]{3,2,1,0:T(8,128)(2,1)} %param.8) | copy-start | bytes 6291460
  6.5 34.1 %all-gather.6.cloned.1.call-start = ((), (), s32[]{:S(2)}) async-start(), calls=%async_computation.3 | async-start | bytes 1572864 | tf_op jit(solution)/shard_map/all_gather | solution.py:35
  7.3 106.4 %all-gather.4.cloned.1.call-start = ((), (), s32[]{:S(2)}) async-start(), calls=%async_computation.2 | async-start | bytes 1572864 | tf_op jit(solution)/shard_map/all_gather | solution.py:35
  42.7 20.8 %copy-start.3 = (bf16[2,1,512,256]{3,2,1,0:T(8,128)(2,1)S(1)}, bf16[2,1,512,256]{3,2,1,0:T(8,128)(2,1)}, u32[]{:S(2)}) copy-start(bf16[2,1,512,256]{3,2,1,0:T(8,128)(2,1)} %param.7) | copy-start | bytes 1572868
  60.7 15.9 %collective-permute-start.1 = (bf16[2,1024,256]{2,1,0:T(8,128)(2,1)}, bf16[2,1024,256]{2,1,0:T(8,128)(2,1)}, u32[]{:S(2)}, u32[]{:S(2)}) collective-permute-start(bf16[2,1024,256]{2,1,0:T(8,128)(2,1)} %bitcast.6), channel_id=1, source_target_pairs={{0,254},{2,0},{4,2},{6,4},{8,6},{10,8},{12,10},{14,12},{16,14},{18... | collective-permute-start | bytes 3145736 | tf_op jit(solution)/shard_map/ppermute | solution.py:15
  62.4 15.3 %collective-permute-start = (bf16[2,1024,256]{2,1,0:T(8,128)(2,1)}, bf16[2,1024,256]{2,1,0:T(8,128)(2,1)}, u32[]{:S(2)}, u32[]{:S(2)}) collective-permute-start(bf16[2,1024,256]{2,1,0:T(8,128)(2,1)} %bitcast.6), channel_id=1, source_target_pairs={{0,2},{2,4},{4,6},{6,8},{8,10},{10,12},{12,14},{14,16},{16,18},{18... | collective-permute-start | bytes 3145736 | tf_op jit(solution)/shard_map/ppermute | solution.py:15
  78.7 3.0 %copy-start.4 = (bf16[2,1,512,1024]{3,2,1,0:T(8,128)(2,1)S(1)}, bf16[2,1,512,1024]{3,2,1,0:T(8,128)(2,1)}, u32[]{:S(2)}) copy-start(bf16[2,1,512,1024]{3,2,1,0:T(8,128)(2,1)} %param.9) | copy-start | bytes 6291460
  134.5 26.3 %collective-permute-start.3 = (bf16[2,1024,256]{2,1,0:T(8,128)(2,1)}, bf16[2,1024,256]{2,1,0:T(8,128)(2,1)}, u32[]{:S(2)}, u32[]{:S(2)}) collective-permute-start(bf16[2,1024,256]{2,1,0:T(8,128)(2,1)} %bitcast.77), channel_id=1, source_target_pairs={{0,252},{2,254},{4,0},{6,2},{8,4},{10,6},{12,8},{14,10},{16,12},{1... | collective-permute-start | bytes 3145736 | tf_op jit(solution)/shard_map/ppermute | solution.py:15
  139.7 27.1 %collective-permute-start.2 = (bf16[2,1024,256]{2,1,0:T(8,128)(2,1)}, bf16[2,1024,256]{2,1,0:T(8,128)(2,1)S(1)}, u32[]{:S(2)}, u32[]{:S(2)}) collective-permute-start(bf16[2,1024,256]{2,1,0:T(8,128)(2,1)} %bitcast.78), channel_id=1, source_target_pairs={{0,4},{2,6},{4,8},{6,10},{8,12},{10,14},{12,16},{14,18},{16,20},{1... | collective-permute-start | bytes 3145736 | tf_op jit(solution)/shard_map/ppermute | solution.py:15
  166.8 3.0 %copy-start.1 = (bf16[2,1,512,1024]{3,2,1,0:T(8,128)(2,1)S(1)}, bf16[2,1,512,1024]{3,2,1,0:T(8,128)(2,1)}, u32[]{:S(2)}) copy-start(bf16[2,1,512,1024]{3,2,1,0:T(8,128)(2,1)} %param.12) | copy-start | bytes 6291460
  166.8 3.0 %copy-start.2 = (bf16[2,512,256]{1,2,0:T(8,128)(2,1)S(1)}, bf16[2,512,256]{1,2,0:T(8,128)(2,1)}, u32[]{:S(2)}) copy-start(bf16[2,512,256]{1,2,0:T(8,128)(2,1)} %fusion.33) | copy-start | bytes 1572868
Sparse Core Ops, SparseCore 0:
  9.1 31.4 all-gather.5
  85.0 28.5 all-gather.3
